TPU v7x, 32 devices: a whole 2x2x4 slice. The times are simulated.
32 devices in a mesh: grp: 2 (over x), chan: 4 (over y, core), ctx: 4 (over z).
Axes of the slice: x: 2, y: 2, z: 4, core: 2. Of those that a mesh axis runs over, the one named last changes fastest.
Arguments:
- features: bfloat16 [4096, 4096], P(('grp', 'ctx'), 'chan'), parts along dimension 0, may hold values from -6 to 6
- filter_taps: bfloat16 [2048, 4096], P(None, 'chan'), may hold values from -0.125 to 0.125
- skip_gain: float32 [4096], P('chan'), may hold values from -4 to 4
- in_weight: bfloat16 [4096, 3, 4096], P(None, None, 'chan'), may hold values from -0.09375 to 0.09375
- out_weight: bfloat16 [4096, 4096], P(None, 'chan'), may hold values from -0.125 to 0.125
Outputs:
- layer_out: bfloat16 [4096, 4096], P(('grp', 'ctx'), 'chan'), parts along dimension 0
There are 2 independent parts, one for each index of `grp`. A program takes and returns all parts, laid end to end along the dimension named above; an argument that names none is the same for every part. Nothing has to cross between parts.
All inputs are finite; a program needn't handle non-finite values.
Results may differ from a plain program's by a relative error of at most 0.013.
Values may be sent and summed in bfloat16 or wider, within the bound.
No kernel may reach another device: no remote copies, remote signals or barrier semaphores. Data moves between devices by JAX's collectives and lax.ppermute only.
A program may use at most 320 MiB of HBM per device.

v0:
```python
import math
import jax
import jax.numpy as jnp
from jax import lax
from jax.sharding import PartitionSpec as P

P_SIZE = 128


def dft_tables(block_len):
    period = 2 * block_len
    freq_col = jnp.arange(period, dtype=jnp.int32)[:, None]
    place_row = jnp.arange(period, dtype=jnp.int32)[None, :]
    angles = (freq_col * place_row % period).astype(jnp.float32) * (2.0 * math.pi / period)
    forward = jnp.concatenate([jnp.cos(angles), -jnp.sin(angles)], axis=0).astype(jnp.bfloat16)
    out_place = jnp.arange(block_len, dtype=jnp.int32)[:, None] + block_len
    angle_out = (out_place * place_row % period).astype(jnp.float32) * (2.0 * math.pi / period)
    inverse = (jnp.concatenate([jnp.cos(angle_out), -jnp.sin(angle_out)], axis=1) / period).astype(
        jnp.bfloat16
    )
    return (forward, inverse)


def input_spectra(token_rows, forward):
    channels = token_rows.shape[1]
    grouped = token_rows.reshape(token_rows.shape[0] // P_SIZE, P_SIZE, channels)
    spectra = jnp.einsum(
        "fp,bpc->bfc", forward[:, :P_SIZE], grouped, preferred_element_type=jnp.float32
    )
    return spectra.astype(jnp.bfloat16)


def segment_spectra(padded, forward):
    channels = padded.shape[1]
    count = padded.shape[0] // P_SIZE - 1
    tap_blocks = padded.reshape(count + 1, P_SIZE, channels)
    segments = jnp.concatenate([tap_blocks[:-1], tap_blocks[1:]], axis=1)
    spectra = jnp.einsum("fn,knc->kfc", forward, segments, preferred_element_type=jnp.float32)
    return spectra.astype(jnp.bfloat16)


def shards(features, filter_taps, skip_gain, in_weight, out_weight):
    forward, inverse = dft_tables(P_SIZE)
    channels = in_weight.shape[2]
    tok_rows = features.shape[0]
    per_dev = tok_rows // P_SIZE
    period = 2 * P_SIZE
    total_blocks = per_dev * lax.axis_size("ctx")
    first_mine = lax.axis_index("ctx") * per_dev
    last_mine = first_mine + per_dev - 1
    padded_all = jnp.concatenate([jnp.zeros((P_SIZE, channels), jnp.bfloat16), filter_taps], axis=0)
    lag_spectra = segment_spectra(padded_all, forward)
    flipped = jnp.concatenate([lag_spectra[::-1], jnp.zeros_like(lag_spectra)], axis=0)
    flat_in = in_weight.reshape(in_weight.shape[0], 3 * channels)
    weight_slice = flat_in
    projected = jnp.dot(
        lax.all_gather(features, "chan", axis=1, tiled=True),
        weight_slice,
        preferred_element_type=jnp.float32,
    )
    query_rows = projected[:, :channels].astype(jnp.bfloat16)
    mixed_in = (projected[:, channels : 2 * channels] * projected[:, 2 * channels :]).astype(
        jnp.bfloat16
    )

    def add_spectra(running, source):
        source_re = source[:, :period].astype(jnp.float32)
        source_im = source[:, period:].astype(jnp.float32)
        outputs = []
        for out_block in range(per_dev):
            start_lag = total_blocks - 1 - (first_mine + out_block)
            window = lax.dynamic_slice_in_dim(flipped, start_lag, source.shape[0], 0).astype(
                jnp.float32
            )
            lag_re = window[:, :period]
            lag_im = window[:, period:]
            out_re = jnp.sum(lag_re * source_re - lag_im * source_im, axis=0)
            out_im = jnp.sum(lag_re * source_im + lag_im * source_re, axis=0)
            outputs.append(jnp.concatenate([out_re, out_im], axis=0))
        return running + jnp.stack(outputs)

    zero_spectra = jnp.zeros((per_dev, 2 * period, channels), jnp.float32)
    portion = lax.all_gather(mixed_in, "ctx", axis=0, tiled=True)
    first_in = jnp.int32(0) // P_SIZE

    def accumulate(current):
        return add_spectra(current, input_spectra(portion, forward))

    summed = lax.cond(first_in <= last_mine, accumulate, lambda current: current, zero_spectra)
    block_spectra = summed.astype(jnp.bfloat16)
    conv_out = jnp.einsum(
        "tf,bfc->btc", inverse, block_spectra, preferred_element_type=jnp.float32
    ).reshape(tok_rows, channels)
    gated_rows = (
        query_rows.astype(jnp.float32)
        * (conv_out + skip_gain[None, :] * mixed_in.astype(jnp.float32))
    ).astype(jnp.bfloat16)
    weight_slice = out_weight
    layer_out = jnp.dot(
        lax.all_gather(gated_rows, "chan", axis=1, tiled=True),
        weight_slice,
        preferred_element_type=jnp.float32,
    )
    return layer_out.astype(jnp.bfloat16)


def solution(mesh):
    return jax.shard_map(
        shards,
        mesh=mesh,
        in_specs=(
            P(("grp", "ctx"), "chan"),
            P(None, "chan"),
            P("chan"),
            P(None, None, "chan"),
            P(None, "chan"),
        ),
        out_specs=P(("grp", "ctx"), "chan"),
        check_vma=False,
    )
```

profile of v0, /device:TPU:0, one launch (start us, length us, event | category | flops | bytes accessed | tf_op | source)
XLA Modules:
  0.0 333.9 jit_solution(129528146827862470)
XLA Ops:
  6.5 0.0 all-gather.4.cloned.1.call-start
  6.5 0.7 all-gather.4.cloned.1.call-update
  7.3 0.0 all-gather.6.cloned.1.call-start
  7.3 31.7 %copy.13 = bf16[4096,3,1024]{0,2,1:T(8,128)(2,1)} copy(bf16[4096,3,1024]{2,0,1:T(8,128)(2,1)} %param.10) | data formatting | bytes 50331648 | tf_op args[3]
  39.0 7.1 %all-gather.4.cloned.1.call-done = bf16[512,4096]{1,0:T(8,128)(2,1)} async-done(((bf16[512,1024]{1,0:T(8,128)(2,1)}), bf16[512,4096]{1,0:T(8,128)(2,1)}) %all-gather.4.cloned.1.call-update) | async-done | bytes 4194320 | tf_op jit(solution)/shard_map/all_gather | solution.py:57
  46.1 17.9 %fusion.50 = f32[512,3072]{1,0:T(8,128)S(1)} fusion(bf16[512,4096]{1,0:T(8,128)(2,1)} %all-gather.4.cloned.1.call-done, bf16[4096,3072]{0,1:T(8,128)(2,1)} %bitcast.39), kind=kOutput, calls=%fused_computation.93 | convolution fusion | flops 12884901888 | bytes 35651584 | tf_op jit(solution)/shard_map/dot_general | solution.py:56
  64.0 0.0 copy-start
  64.0 2.6 copy-done
  66.6 1.3 fusion.25
  67.9 0.0 all-gather.6.cloned.1.call-update
  67.9 0.0 all-gather.8.cloned.1.call-start
  67.9 4.5 %pad_slice_fusion = bf16[2048,1024]{1,0:T(8,128)(2,1)} fusion(bf16[2048,1024]{1,0:T(8,128)(2,1)} %param.8), kind=kLoop, calls=%fused_computation.52 | loop fusion | bytes 8388608 | tf_op jit(solution)/shard_map/slice | solution.py:37
  72.4 6.5 %copy.14 = bf16[16,128,1024]{1,2,0:T(8,128)(2,1)} copy(bf16[16,128,1024]{2,1,0:T(8,128)(2,1)} %bitcast.41) | data formatting | bytes 8388608 | tf_op jit(solution)/shard_map/slice | solution.py:37
  78.9 6.4 %copy.15 = bf16[16,128,1024]{1,2,0:T(8,128)(2,1)} copy(bf16[16,128,1024]{2,1,0:T(8,128)(2,1)} %bitcast.40) | data formatting | bytes 8388608 | tf_op jit(solution)/shard_map/slice | solution.py:37
  85.3 1.1 negate_convert_fusion
  86.4 10.4 %convert_bitcast_fusion.1 = bf16[16,512,1024]{1,2,0:T(8,128)(2,1)} fusion(bf16[16,128,1024]{1,2,0:T(8,128)(2,1)} %copy.15, bf16[16,128,1024]{1,2,0:T(8,128)(2,1)} %copy.14, bf16[256,256]{1,0:T(8,128)(2,1)S(1)} %get-tuple-element.49, bf16[256,256]{1,0:T(8,128)(2,1)S(1)} %get-tuple-element.50), kind=kOutput, calls=%fused_computation.48 | convolution fusion | flops 4320657408 | bytes 25427968 | tf_op jit(solution)/shard_map/fn,knc->kfc/dot_general | solution.py:38
  96.8 13.8 %rev.3 = bf16[16,512,1024]{1,2,0:T(8,128)(2,1)} reverse(bf16[16,512,1024]{1,2,0:T(8,128)(2,1)} %convert_bitcast_fusion.1), dimensions={0} | reverse | bytes 33554432 | tf_op jit(solution)/shard_map/rev | solution.py:53
  110.6 1.2 fusion.46
  111.8 36.9 %all-gather.6.cloned.1.call-done = bf16[2048,1024]{1,0:T(8,128)(2,1)} async-done(((bf16[512,1024]{1,0:T(8,128)(2,1)}), bf16[2048,1024]{1,0:T(8,128)(2,1)}) %all-gather.6.cloned.1.call-update) | async-done | bytes 4194320 | tf_op jit(solution)/shard_map/all_gather | solution.py:83
  148.8 110.0 %conditional.1 = (bf16[4,512,1024]{1,2,0:T(8,128)(2,1)}) conditional(s32[]{:T(128)} %convert_element_type.68, () %tuple.13, (bf16[16,512,1024]{1,2,0:T(8,128)(2,1)}, s32[]{:T(128)}, bf16[2048,1024]{1,0:T(8,128)(2,1)}, bf16[512,256]{1,0:T(8,128)(2,1)S(1)}) %tuple.14), branch_computations={%region_0.1_spmd, %region_1.10_spmd} | conditional | flops 2344615936 | bytes 344064256 | solution.py:89
  148.8 45.6 %fusion.18 = (f32[16,512,1024]{1,2,0:T(8,128)}, f32[16,512,1024]{1,2,0:T(8,128)}, f32[16,512,1024]{1,2,0:T(8,128)}, f32[16,512,1024]{1,2,0:T(8,128)}) fusion(s32[]{:T(128)S(6)} %select_n.25, bf16[16,512,1024]{1,2,0:T(8,128)(2,1)} %get-tuple-element.19, s32[]{:T(128)S(6)} %select_n.24, s32[]{:T(128)S(6)} %select_n.26, s32[]{:T(128)S(6)} %select_n.23), kind=kLoop, calls=%fused_computation.38 | loop fusion | flops 33554432 | bytes 150994960 | tf_op jit(solution)/shard_map/cond/branch_1_fun/convert_element_type | solution.py:72
  194.3 10.4 %convert_bitcast_fusion = bf16[16,512,1024]{1,2,0:T(8,128)(2,1)} fusion(bf16[16,128,1024]{2,1,0:T(8,128)(2,1)} %bitcast.42, bf16[512,256]{1,0:T(8,128)(2,1)S(1)} %get-tuple-element.22), kind=kOutput, calls=%fused_computation.40 | convolution fusion | flops 2155872256 | bytes 21102592 | tf_op jit(solution)/shard_map/cond/branch_1_fun/fp,bpc->bfc/dot_general | solution.py:27
  204.8 49.9 %fusion.5 = (bf16[256,1024]{0,1:T(8,128)(2,1)S(1)}, bf16[256,1024]{0,1:T(8,128)(2,1)S(1)}, bf16[256,1024]{0,1:T(8,128)(2,1)S(1)}, bf16[256,1024]{0,1:T(8,128)(2,...) fusion(f32[16,512,1024]{1,2,0:T(8,128)} %get-tuple-element.40, ...), kind=kLoop, calls=%fused_computation.25 | loop fusion | flops 140509184 | bytes 155189248 | tf_op jit(solution)/shard_map/cond/branch_1_fun/reduce_sum | solution.py:77
  254.7 1.4 maximum_bitcast_fusion
  256.1 0.2 maximum_bitcast_fusion.2
  256.3 2.5 pad_maximum_fusion
  258.7 3.7 %fusion.40 = f32[4,1024,128]{1,2,0:T(8,128)S(1)} fusion(bf16[4,512,1024]{1,2,0:T(8,128)(2,1)} %get-tuple-element.51, f32[128,256]{1,0:T(8,128)} %get-tuple-element.48, f32[128,256]{1,0:T(8,128)S(1)} %get-tuple-element.47), kind=kOutput, calls=%fused_computation.82 | convolution fusion | flops 537067520 | bytes 6553600 | tf_op jit(solution)/shard_map/tf,bfc->btc/dot_general | solution.py:91
  262.4 0.0 copy-done.1
  262.4 4.7 %fusion.27 = bf16[512,1024]{1,0:T(8,128)(2,1)} fusion(f32[4,1024,128]{1,2,0:T(8,128)S(1)} %fusion.40, f32[512,3072]{1,0:T(8,128)} %copy-done, f32[1024]{0:T(1024)S(1)} %copy-done.1), kind=kLoop, calls=%fused_computation.58 | loop fusion | flops 4194304 | bytes 8392704 | tf_op jit(solution)/shard_map/convert_element_type | solution.py:97
  267.1 0.0 all-gather.8.cloned.1.call-update
  267.1 50.1 %all-gather.8.cloned.1.call-done = bf16[512,4096]{1,0:T(8,128)(2,1)} async-done(((bf16[512,1024]{1,0:T(8,128)(2,1)}), bf16[512,4096]{1,0:T(8,128)(2,1)}) %all-gather.8.cloned.1.call-update) | async-done | bytes 4194320 | tf_op jit(solution)/shard_map/all_gather | solution.py:100
  317.2 10.1 %convolution_convert_fusion = bf16[512,1024]{1,0:T(8,128)(2,1)} fusion(bf16[512,4096]{1,0:T(8,128)(2,1)} %all-gather.8.cloned.1.call-done, bf16[4096,1024]{1,0:T(8,128)(2,1)} %param.11), kind=kOutput, calls=%fused_computation.59 | convolution fusion | flops 4295491584 | bytes 13631488 | tf_op jit(solution)/shard_map/dot_general | solution.py:99
  (3 shorter events, 0.0 us)
Async XLA Ops:
  6.5 39.6 %all-gather.4.cloned.1.call-start = ((), (), s32[]{:S(2)}) async-start(), calls=%async_computation | async-start | bytes 5242880 | tf_op jit(solution)/shard_map/all_gather | solution.py:57
  7.3 141.5 %all-gather.6.cloned.1.call-start = ((), (), s32[]{:S(2)}) async-start(), calls=%async_computation.1 | async-start | bytes 5242880 | tf_op jit(solution)/shard_map/all_gather | solution.py:83
  64.0 2.6 copy-start
  67.9 249.4 %all-gather.8.cloned.1.call-start = ((), (), s32[]{:S(2)}) async-start(), calls=%async_computation.2 | async-start | bytes 5242880 | tf_op jit(solution)/shard_map/all_gather | solution.py:100
  258.7 3.7 %copy-start.1 = (f32[1024]{0:T(1024)S(1)}, f32[1024]{0:T(1024)}, u32[]{:S(2)}) copy-start(f32[1024]{0:T(1024)} %param.9) | copy-start | bytes 12292
Sparse Core Ops, SparseCore 0:
  8.9 37.1 all-gather.3
  68.0 80.7 all-gather.5
  267.3 49.9 all-gather.7
where the time goes:
time: 335 us; the launch traced here: 334 us
  other arithmetic  108 us (32%)
  waiting for transfers between devices  94.9 us (28%)
  local copies, waits for them, and re-layouts  65.4 us (20%)
  matrix products  52.5 us (16%)
  between operations  13.2 us (4%)
    all_gather x1, waiting for transfers between devices, shards(): lax.all_gather(gated_rows, 'chan', axis=1, tiled=True)  50.1 us
    reduce_sum x1, other arithmetic, add_spectra(): out_re = jnp.sum(lag_re * source_re - lag_im * source_im, axis=0)  49.9 us
    convert_element_type x1, other arithmetic, add_spectra(): lax.dynamic_slice_in_dim(flipped, start_lag, source.shape[0], 0)  45.6 us
    all_gather x1, waiting for transfers between devices, shards(): portion = lax.all_gather(mixed_in, 'ctx', axis=0, tiled=True)  36.9 us
    unnamed x5, local copies, waits for them, and re-layouts  34.3 us
    dot_general x1, matrix products, shards(): jnp.dot(lax.all_gather(features, 'chan', axis=1, tiled=True), weight_slic...  17.9 us
    slice x3, local copies, waits for them, and re-layouts, segment_spectra(): segments = jnp.concatenate([tap_blocks[:-1], tap_blocks[1:]], axis=1)  17.3 us
    rev x1, local copies, waits for them, and re-layouts, shards(): lag_spectra[::-1]  13.8 us
  transfers between devices with their start and end apart: 3, of which 3 were waited for; matrix products, arithmetic and copies ran while one was open for 23% of the time, Pallas kernels for 0%

commit v1 on v0

--- a/solution.py
+++ b/solution.py
@@ -80,7 +80,12 @@
         return running + jnp.stack(outputs)
 
     zero_spectra = jnp.zeros((per_dev, 2 * period, channels), jnp.float32)
-    portion = lax.all_gather(mixed_in, "ctx", axis=0, tiled=True)
+    ring = [mixed_in]
+    for hop in range(3):
+        ring.append(lax.ppermute(ring[-1], "ctx", [(dev, (dev + 1) % 4) for dev in range(4)]))
+    portion = jnp.roll(
+        jnp.concatenate(ring[::-1], axis=0), (lax.axis_index("ctx") + 1) * ring[0].shape[0], axis=0
+    )
     first_in = jnp.int32(0) // P_SIZE
 
     def accumulate(current):

time: 335 us -> 354 us (1.057)
  local copies, waits for them, and re-layouts: 65.4 us -> 77.4 us
  other arithmetic: 108 us -> 112 us
    all_gather x1 -> x0, waiting for transfers between devices: 36.9 us -> none  [shards(): portion = lax.all_gather(mixed_in, 'ctx', axis=0, tiled=True)]
    ppermute x0 -> x3, waiting for transfers between devices: none -> 35.8 us  [shards(): lax.ppermute(ring[-1], 'ctx', [(dev, (dev + 1) % 4) for dev in range(4)])]
    unnamed x5 -> x17, local copies, waits for them, and re-layouts: 34.3 us -> 43.1 us
    dynamic_slice x0 -> x1, local copies, waits for them, and re-layouts: none -> 5.4 us  [shards(): jnp.roll(jnp.concatenate(ring[::-1], axis=0), (lax.axis_index('ctx') + 1)...]
    unnamed x0 -> x2, other arithmetic: none -> 3.71 us
  transfers between devices with their start and end apart: 3 -> 5, of which waited for: 3 -> 5; matrix products, arithmetic and copies ran while one was open for 23% -> 21% of each run, Pallas kernels for 0% -> 0%
where the time goes in v1:
time: 354 us; the launch traced here: 353 us
  other arithmetic  112 us (32%)
  waiting for transfers between devices  95.7 us (27%)
  local copies, waits for them, and re-layouts  77.4 us (22%)
  matrix products  52.5 us (15%)
  between operations  13.5 us (4%)
    all_gather x1, waiting for transfers between devices, shards(): lax.all_gather(gated_rows, 'chan', axis=1, tiled=True)  52.1 us
    reduce_sum x1, other arithmetic, add_spectra(): out_re = jnp.sum(lag_re * source_re - lag_im * source_im, axis=0)  50.2 us
    convert_element_type x1, other arithmetic, add_spectra(): lax.dynamic_slice_in_dim(flipped, start_lag, source.shape[0], 0)  45.5 us
    unnamed x17, local copies, waits for them, and re-layouts  43.1 us
    ppermute x3, waiting for transfers between devices, shards(): lax.ppermute(ring[-1], 'ctx', [(dev, (dev + 1) % 4) for dev in range(4)])  35.8 us
    dot_general x1, matrix products, shards(): jnp.dot(lax.all_gather(features, 'chan', axis=1, tiled=True), weight_slic...  18 us
    slice x3, local copies, waits for them, and re-layouts, segment_spectra(): segments = jnp.concatenate([tap_blocks[:-1], tap_blocks[1:]], axis=1)  15.2 us
    rev x1, local copies, waits for them, and re-layouts, shards(): lag_spectra[::-1]  13.7 us
  transfers between devices with their start and end apart: 5, of which 5 were waited for; matrix products, arithmetic and copies ran while one was open for 21% of the time, Pallas kernels for 0%

profile of v1, /device:TPU:0, one launch (start us, length us, event | category | flops | bytes accessed | tf_op | source)
XLA Modules:
  0.0 352.6 jit_solution(5538351282623654144)
XLA Ops:
  7.3 31.6 %copy.12 = bf16[4096,3,1024]{0,2,1:T(8,128)(2,1)} copy(bf16[4096,3,1024]{2,0,1:T(8,128)(2,1)} %param.10) | data formatting | bytes 50331648 | tf_op args[3]
  38.9 7.2 %all-gather.3.cloned.1.call-done = bf16[512,4096]{1,0:T(8,128)(2,1)} async-done(((bf16[512,1024]{1,0:T(8,128)(2,1)}), bf16[512,4096]{1,0:T(8,128)(2,1)}) %all-gather.3.cloned.1.call-update) | async-done | bytes 4194320 | tf_op jit(solution)/shard_map/all_gather | solution.py:57
  46.1 18.0 %fusion.50 = f32[512,3072]{1,0:T(8,128)S(1)} fusion(bf16[512,4096]{1,0:T(8,128)(2,1)} %all-gather.3.cloned.1.call-done, bf16[4096,3072]{0,1:T(8,128)(2,1)} %bitcast.41), kind=kOutput, calls=%fused_computation.102 | convolution fusion | flops 12884901888 | bytes 35651584 | tf_op jit(solution)/shard_map/dot_general | solution.py:56
  64.1 2.7 copy-done
  67.2 1.5 collective-permute-start
  68.7 25.6 %collective-permute-done = bf16[512,1024]{1,0:T(8,128)(2,1)S(1)} collective-permute-done((bf16[512,1024]{1,0:T(8,128)(2,1)S(1)}, bf16[512,1024]{1,0:T(8,128)(2,1)S(1)}, u32[]{:S(2)}, u32[]{:S(2)}) %collective-permute-start) | collective-permute-done | bytes 1048608 | tf_op jit(solution)/shard_map/ppermute | solution.py:85
  94.3 2.4 pad_slice_fusion
  96.7 6.4 %copy.13 = bf16[16,128,1024]{1,2,0:T(8,128)(2,1)} copy(bf16[16,128,1024]{2,1,0:T(8,128)(2,1)} %bitcast.44) | data formatting | bytes 8388608 | tf_op jit(solution)/shard_map/slice | solution.py:37
  103.1 6.4 %copy.14 = bf16[16,128,1024]{1,2,0:T(8,128)(2,1)} copy(bf16[16,128,1024]{2,1,0:T(8,128)(2,1)} %bitcast.43) | data formatting | bytes 8388608 | tf_op jit(solution)/shard_map/slice | solution.py:37
  109.5 1.1 negate_convert_fusion
  110.6 10.0 %collective-permute-done.1 = bf16[512,1024]{1,0:T(8,128)(2,1)S(1)} collective-permute-done((bf16[512,1024]{1,0:T(8,128)(2,1)S(1)}, bf16[512,1024]{1,0:T(8,128)(2,1)S(1)}, u32[]{:S(2)}, u32[]{:S(2)}) %collective-permute-start.1) | collective-permute-done | bytes 1048608 | tf_op jit(solution)/shard_map/ppermute | solution.py:85
  120.6 10.3 %convert_bitcast_fusion.1 = bf16[16,512,1024]{1,2,0:T(8,128)(2,1)} fusion(bf16[16,128,1024]{1,2,0:T(8,128)(2,1)} %copy.14, bf16[16,128,1024]{1,2,0:T(8,128)(2,1)} %copy.13, bf16[256,256]{1,0:T(8,128)(2,1)S(1)} %get-tuple-element.166, bf16[256,256]{1,0:T(8,128)(2,1)S(1)} %get-tuple-element.167), kind=kOutput, calls=%fused_computation.49 | convolution fusion | flops 4320657408 | bytes 25427968 | tf_op jit(solution)/shard_map/fn,knc->kfc/dot_general | solution.py:38
  130.9 13.7 %rev.3 = bf16[16,512,1024]{1,2,0:T(8,128)(2,1)} reverse(bf16[16,512,1024]{1,2,0:T(8,128)(2,1)} %convert_bitcast_fusion.1), dimensions={0} | reverse | bytes 33554432 | tf_op jit(solution)/shard_map/rev | solution.py:53
  144.6 1.2 fusion.46
  146.0 2.3 constant_dynamic-update-slice_fusion.7
  148.3 1.1 constant_dynamic-update-slice_fusion.6
  149.4 1.1 constant_dynamic-update-slice_fusion.5
  150.4 3.7 %constant_dynamic-update-slice_fusion.4 = bf16[4096,1024]{1,0:T(8,128)(2,1)} fusion(bf16[4096,1024]{1,0:T(8,128)(2,1)} %constant_dynamic-update-slice_fusion.5, f32[512,3072]{1,0:T(8,128)} %copy-done), kind=kLoop, calls=%fused_computation.94 | loop fusion | flops 1048576 | bytes 5242880
  154.1 2.3 constant_dynamic-update-slice_fusion.3
  157.4 1.1 constant_dynamic-update-slice_fusion.1
  158.5 1.3 constant_dynamic-update-slice_fusion
  159.8 115.3 %conditional.1 = (bf16[4,512,1024]{1,2,0:T(8,128)(2,1)}) conditional(s32[]{:T(128)} %convert_element_type.92, () %tuple.24, (bf16[16,512,1024]{1,2,0:T(8,128)(2,1)}, s32[]{:T(128)}, s32[]{:T(128)}, s32[]{:T(128)}, bf16[4096,1024]{1,0:T(8,128)(2,1)}, /*index=5*/bf16[512,256]{1,0:T(8,128)(2,1)S(1)}, s32[]{:T(128)}, s32[]{:T(128)}) %tuple.28), branch_computations={%region_0.1_spmd, %region_1.10_spmd.clone} | conditional | flops 2344615936 | bytes 352453056 | solution.py:94
  159.8 5.4 %constant_dynamic-slice_fusion = bf16[2048,1024]{1,0:T(8,128)(2,1)} fusion(bf16[4096,1024]{1,0:T(8,128)(2,1)} %get-tuple-element.124, s32[]{:T(128)S(6)} %select_n.66), kind=kLoop, calls=%fused_computation.48 | loop fusion | bytes 8388612 | tf_op jit(solution)/shard_map/jit(_roll_dynamic)/dynamic_slice | solution.py:86
  165.2 10.4 %convert_bitcast_fusion = bf16[16,512,1024]{1,2,0:T(8,128)(2,1)} fusion(bf16[16,128,1024]{2,1,0:T(8,128)(2,1)} %bitcast.42, bf16[512,256]{1,0:T(8,128)(2,1)S(1)} %get-tuple-element.126), kind=kOutput, calls=%fused_computation.40 | convolution fusion | flops 2155872256 | bytes 21102592 | tf_op jit(solution)/shard_map/cond/branch_1_fun/fp,bpc->bfc/dot_general | solution.py:27
  175.7 45.5 %fusion.18 = (f32[16,512,1024]{1,2,0:T(8,128)}, f32[16,512,1024]{1,2,0:T(8,128)}, f32[16,512,1024]{1,2,0:T(8,128)}, f32[16,512,1024]{1,2,0:T(8,128)}) fusion(s32[]{:T(128)S(6)} %select_n.68, bf16[16,512,1024]{1,2,0:T(8,128)(2,1)} %get-tuple-element.122, s32[]{:T(128)S(6)} %select_n.67, s32[]{:T(128)S(6)} %select_n.69, s32[]{:T(128)S(6)} %select_n.64), kind=kLoop, calls=%fused_computation.38 | loop fusion | flops 33554432 | bytes 150994960 | tf_op jit(solution)/shard_map/cond/branch_1_fun/convert_element_type | solution.py:72
  221.2 50.2 %fusion.5 = (bf16[256,1024]{0,1:T(8,128)(2,1)S(1)}, bf16[256,1024]{0,1:T(8,128)(2,1)S(1)}, bf16[256,1024]{0,1:T(8,128)(2,1)S(1)}, bf16[256,1024]{0,1:T(8,128)(2,...) fusion(f32[16,512,1024]{1,2,0:T(8,128)} %get-tuple-element.157,, ...), kind=kLoop, calls=%fused_computation.25 | loop fusion | flops 140509184 | bytes 155189248 | tf_op jit(solution)/shard_map/cond/branch_1_fun/reduce_sum | solution.py:77
  271.4 1.4 maximum_bitcast_fusion
  272.9 2.2 pad_maximum_fusion
  275.1 3.7 %fusion.40 = f32[4,1024,128]{1,2,0:T(8,128)S(1)} fusion(bf16[4,512,1024]{1,2,0:T(8,128)(2,1)} %get-tuple-element.168, f32[128,256]{1,0:T(8,128)} %get-tuple-element.165, f32[128,256]{1,0:T(8,128)S(1)} %get-tuple-element.164), kind=kOutput, calls=%fused_computation.83 | convolution fusion | flops 537067520 | bytes 6553600 | tf_op jit(solution)/shard_map/tf,bfc->btc/dot_general | solution.py:96
  278.8 4.7 %fusion.27 = bf16[512,1024]{1,0:T(8,128)(2,1)} fusion(f32[4,1024,128]{1,2,0:T(8,128)S(1)} %fusion.40, f32[512,3072]{1,0:T(8,128)} %copy-done, f32[1024]{0:T(1024)S(1)} %copy-done.2), kind=kLoop, calls=%fused_computation.59 | loop fusion | flops 4194304 | bytes 8392704 | tf_op jit(solution)/shard_map/convert_element_type | solution.py:102
  283.5 52.1 %all-gather.5.cloned.1.call-done = bf16[512,4096]{1,0:T(8,128)(2,1)} async-done(((bf16[512,1024]{1,0:T(8,128)(2,1)}), bf16[512,4096]{1,0:T(8,128)(2,1)}) %all-gather.5.cloned.1.call-update) | async-done | bytes 4194320 | tf_op jit(solution)/shard_map/all_gather | solution.py:105
  335.6 10.1 %convolution_convert_fusion = bf16[512,1024]{1,0:T(8,128)(2,1)} fusion(bf16[512,4096]{1,0:T(8,128)(2,1)} %all-gather.5.cloned.1.call-done, bf16[4096,1024]{1,0:T(8,128)(2,1)} %param.11), kind=kOutput, calls=%fused_computation.60 | convolution fusion | flops 4295491584 | bytes 13631488 | tf_op jit(solution)/shard_map/dot_general | solution.py:104
  (22 shorter events, 2.5 us)
Async XLA Ops:
  6.5 39.6 %all-gather.3.cloned.1.call-start = ((), (), s32[]{:S(2)}) async-start(), calls=%async_computation | async-start | bytes 5242880 | tf_op jit(solution)/shard_map/all_gather | solution.py:57
  7.3 328.4 %all-gather.5.cloned.1.call-start = ((), (), s32[]{:S(2)}) async-start(), calls=%async_computation.1 | async-start | bytes 5242880 | tf_op jit(solution)/shard_map/all_gather | solution.py:105
  46.1 48.2 %copy-start.1 = (bf16[2048,1024]{1,0:T(8,128)(2,1)S(1)}, bf16[2048,1024]{1,0:T(8,128)(2,1)}, u32[]{:S(2)}) copy-start(bf16[2048,1024]{1,0:T(8,128)(2,1)} %param.8) | copy-start | bytes 12582916
  64.1 2.7 copy-start
  67.2 27.2 %collective-permute-start = (bf16[512,1024]{1,0:T(8,128)(2,1)S(1)}, bf16[512,1024]{1,0:T(8,128)(2,1)S(1)}, u32[]{:S(2)}, u32[]{:S(2)}) collective-permute-start(bf16[512,1024]{1,0:T(8,128)(2,1)S(1)} %fusion.25), channel_id=1, source_target_pairs={{0,1},{1,2},{2,3},{3,0},{4,5},{5,6},{6,7},{7,4},{8,9},{9,10},{10,1... | collective-permute-start | bytes 3145736 | tf_op jit(solution)/shard_map/ppermute | solution.py:85
  94.3 26.2 %collective-permute-start.1 = (bf16[512,1024]{1,0:T(8,128)(2,1)S(1)}, bf16[512,1024]{1,0:T(8,128)(2,1)S(1)}, u32[]{:S(2)}, u32[]{:S(2)}) collective-permute-start(bf16[512,1024]{1,0:T(8,128)(2,1)S(1)} %collective-permute-done), channel_id=1, source_target_pairs={{0,1},{1,2},{2,3},{3,0},{4,5},{5,6},{6,7},{7,4},{8,9},{9,10},{10,1... | collective-permute-start | bytes 3145736 | tf_op jit(solution)/shard_map/ppermute | solution.py:85
  120.6 25.5 %collective-permute-start.2 = (bf16[512,1024]{1,0:T(8,128)(2,1)S(1)}, bf16[512,1024]{1,0:T(8,128)(2,1)}, u32[]{:S(2)}, u32[]{:S(2)}) collective-permute-start(bf16[512,1024]{1,0:T(8,128)(2,1)S(1)} %collective-permute-done.1), channel_id=1, source_target_pairs={{0,1},{1,2},{2,3},{3,0},{4,5},{5,6},{6,7},{7,4},{8,9},{9,10},{10,1... | collective-permute-start | bytes 3145736 | tf_op jit(solution)/shard_map/ppermute | solution.py:85
  148.3 10.2 %slice-start = ((s8[6291456]{0:T(1024)(128)(4,1)}), s8[4194304]{0:T(1024)(128)(4,1)S(1)}, s32[]{:S(2)}) async-start(s8[6291456]{0:T(1024)(128)(4,1)} %bitcast.39), calls=%async_computation.2 | async-start | bytes 8388608
  150.4 8.1 %slice-start.1 = ((s8[6291456]{0:T(1024)(128)(4,1)}), s8[2097152]{0:T(1024)(128)(4,1)S(1)}, s32[]{:S(2)}) async-start(s8[6291456]{0:T(1024)(128)(4,1)} %bitcast.39), calls=%async_computation.3 | async-start | bytes 4194304
  275.1 3.7 %copy-start.2 = (f32[1024]{0:T(1024)S(1)}, f32[1024]{0:T(1024)}, u32[]{:S(2)}) copy-start(f32[1024]{0:T(1024)} %param.9) | copy-start | bytes 12292
Sparse Core Ops, SparseCore 0:
  8.9 37.1 all-gather.2
  283.7 51.9 all-gather.4
